TPU v7x, 32 devices: a whole 2x2x4 slice. The times are simulated.
32 devices in a mesh: groups: 2 (over x), expert: 16 (over z, y, core).
Axes of the slice: x: 2, y: 2, z: 4, core: 2. Of those that a mesh axis runs over, the one named last changes fastest.
Arguments:
- tokens: bfloat16 [8192, 1024], P(('groups', 'expert')), parts along dimension 0, may hold values from -6 to 6
- routes: int32 [8192, 2], P(('groups', 'expert')), parts along dimension 0, may hold values from 0 to 7, all different within a row; in each aligned block of 256 rows (0 to 255, 256 to 511, ...) at most 128 rows name the same one
- gates: float32 [8192, 2], P(('groups', 'expert')), parts along dimension 0, may hold values from 0.2 to 1
- w_in: bfloat16 [16, 1024, 2048], P('expert'), may hold values from -0.1875 to 0.1875
- w_down: bfloat16 [16, 1024, 1024], P('expert'), may hold values from -0.125 to 0.125
Outputs:
- mixed: bfloat16 [8192, 1024], P(('groups', 'expert')), parts along dimension 0
There are 2 independent parts, one for each index of `groups`. A program takes and returns all parts, laid end to end along the dimension named above; an argument that names none is the same for every part. Nothing has to cross between parts.
Inputs may be any that keep to these rules, and one draw needn't show every extreme that they name: `routes`: each row names 2 different experts; in the 256 rows of one device no expert is named by more than 128 rows, and exactly 128 for some expert in some device's rows.
All inputs are finite; a program needn't handle non-finite values.
Results may differ from a plain program's by a relative error of at most 0.005.
Values may be sent and summed in bfloat16 or wider, within the bound.
No kernel may reach another device: no remote copies, remote signals or barrier semaphores. Data moves between devices by JAX's collectives and lax.ppermute only.
A program may use at most 64 MiB of HBM per device.

v0:
```python
import functools
import jax
import jax.numpy as jnp
from jax import lax
from jax.experimental import pallas as pl
from jax.experimental.pallas import tpu as pltpu
from jax.sharding import PartitionSpec as P


F32 = jnp.float32
BF16 = jnp.bfloat16
BACK_WIDTHS = (4, 4)
ANY = pl.BlockSpec(memory_space=pl.ANY)
HBM = pl.BlockSpec(memory_space=pltpu.HBM)
VMEM = pl.BlockSpec(memory_space=pltpu.VMEM)
PARAMS = pltpu.CompilerParams(vmem_limit_bytes=16 << 20)


def on_chip(x):
    return pltpu.with_memory_space_constraint(x, pltpu.VMEM)


def off_chip(x):
    return pltpu.with_memory_space_constraint(x, pltpu.HBM)


def spans(widths, features):
    unit = features // sum(widths)
    edges = [unit * sum(widths[:i]) for i in range(len(widths) + 1)]
    return list(zip(edges[:-1], edges[1:]))


def cost(flops, moved):
    return pl.CostEstimate(flops=flops, transcendentals=0, bytes_accessed=moved)


def iota(shape, dim):
    return lax.broadcasted_iota(jnp.int32, shape, dim)


def slot_rows(routes, experts, cap):
    count = routes.shape[1]
    first, second = routes[0:1, :], routes[1:2, :]
    ids = iota((experts, count), 0)
    is_first, is_second = ids == first, ids == second
    named = jnp.where(is_first | is_second, 1.0, 0.0).astype(BF16)
    before = jnp.where(iota((count, count), 0) < iota((count, count), 1), 1.0, 0.0).astype(BF16)
    ranks = jnp.dot(named, before, preferred_element_type=F32)
    rank_first = jnp.sum(jnp.where(is_first, ranks, 0.0), axis=0, keepdims=True)
    rank_second = jnp.sum(jnp.where(is_second, ranks, 0.0), axis=0, keepdims=True)
    return first * cap + rank_first.astype(jnp.int32), second * cap + rank_second.astype(jnp.int32)


class Plan:
    def __init__(self, devices, tok_rows):
        self.devices = devices
        self.experts = devices // 2
        self.cap = min(tok_rows, 4 * tok_rows // self.experts)
        self.near = self.experts // 2
        self.direct = self.near <= 8
        self.pieces = self.near if self.direct else 1
        self.slots = self.near * self.cap
        self.piece_rows = self.slots // self.pieces

    def bases(self):
        me = lax.axis_index("expert")
        chip = me // 2
        half_first = chip // self.near * self.near
        if not self.direct:
            return [half_first * self.cap]
        return [(half_first + ((chip % self.near) ^ j)) * self.cap for j in range(self.pieces)]

    def across(self, x):
        return lax.ppermute(x, "expert", [(i, i ^ self.devices // 2) for i in range(self.devices)])

    def partner(self, x):
        return lax.ppermute(x, "expert", [(i, i ^ 1) for i in range(self.devices)])

    def near_exchange(self, parts):
        if self.direct:
            return [parts[0]] + [
                lax.ppermute(parts[j], "expert", [(i, i ^ 2 * j) for i in range(self.devices)])
                for j in range(1, self.pieces)
            ]
        groups = [
            [2 * (half * self.near + chip) + core for chip in range(self.near)]
            for half in range(2)
            for core in range(2)
        ]
        return [lax.all_to_all(parts[0], "expert", split_axis=0, concat_axis=0, tiled=True, axis_index_groups=groups)]


def picks(plan, first, second):
    slots = iota((plan.piece_rows, first.shape[1]), 0)
    return [
        jnp.where((slots == first - base) | (slots == second - base), 1.0, 0.0).astype(BF16)
        for base in plan.bases()
    ]


def gate_pair(plan, first, second, gates):
    count = first.shape[1]
    rows = jnp.concatenate([first.astype(F32), second.astype(F32), gates, jnp.zeros((124, count), F32)], axis=0)
    columns = rows.T
    first_col = columns[:, 0:1].astype(jnp.int32)
    second_col = columns[:, 1:2].astype(jnp.int32)
    slots = iota((count, plan.piece_rows), 1)
    spread = jnp.concatenate(
        [
            jnp.where(slots == first_col - base, columns[:, 2:3], 0.0)
            + jnp.where(slots == second_col - base, columns[:, 3:4], 0.0)
            for base in plan.bases()
        ],
        axis=1,
    )
    high = spread.astype(BF16)
    return high, (spread - high.astype(F32)).astype(BF16)


def stage_body(count, *refs):
    sources, outs, sem = refs[:count], refs[count + 1 : 2 * count + 1], refs[-1]
    copies = [pltpu.make_async_copy(sources[i], outs[i], sem.at[i]) for i in range(count)]
    for copy in copies:
        copy.start()
    for copy in copies:
        copy.wait()


def stage(arrays, after):
    return pl.pallas_call(
        functools.partial(stage_body, len(arrays)),
        in_specs=[HBM] * len(arrays) + [ANY],
        out_specs=[VMEM] * len(arrays),
        out_shape=[pltpu.VMEM(x.shape, x.dtype) for x in arrays],
        scratch_shapes=[pltpu.SemaphoreType.DMA((len(arrays),))],
        cost_estimate=cost(0, sum(2 * x.size * x.dtype.itemsize for x in arrays)),
        compiler_params=PARAMS,
        name="stage",
    )(*[off_chip(x) for x in arrays], after)


def select_body(plan, routes_ref, tokens_ref, *refs):
    out_refs, (routes_vmem, tokens_vmem, sem) = refs[:-3], refs[-3:]
    copies = [
        pltpu.make_async_copy(routes_ref, routes_vmem, sem.at[0]),
        pltpu.make_async_copy(tokens_ref, tokens_vmem, sem.at[1]),
    ]
    for copy in copies:
        copy.start()
    copies[0].wait()
    first, second = slot_rows(routes_vmem[...], plan.experts, plan.cap)
    copies[1].wait()
    tokens = tokens_vmem[...]
    for pick, out_ref in zip(picks(plan, first, second), out_refs):
        out_ref[...] = jnp.dot(pick, tokens, preferred_element_type=F32).astype(BF16)


def select(plan, routes, tokens):
    count, features = tokens.shape
    return pl.pallas_call(
        functools.partial(select_body, plan),
        in_specs=[HBM] * 2,
        out_specs=[VMEM] * plan.pieces,
        out_shape=[pltpu.VMEM((plan.piece_rows, features), BF16)] * plan.pieces,
        scratch_shapes=[
            pltpu.VMEM(routes.shape, routes.dtype),
            pltpu.VMEM(tokens.shape, tokens.dtype),
            pltpu.SemaphoreType.DMA((2,)),
        ],
        cost_estimate=cost(2 * plan.slots * count * features, 2 * plan.slots * features),
        compiler_params=PARAMS,
        name="select",
    )(off_chip(routes), off_chip(tokens))


def far_picks_body(plan, routes_ref, after_ref, pick_ref):
    first, second = slot_rows(routes_ref[...], plan.experts, plan.cap)
    pick_ref[...] = jnp.concatenate(picks(plan, first, second), axis=0)


def far_picks(plan, routes, after):
    count = routes.shape[1]
    return pl.pallas_call(
        functools.partial(far_picks_body, plan),
        in_specs=[VMEM, ANY],
        out_specs=VMEM,
        out_shape=pltpu.VMEM((plan.slots, count), BF16),
        cost_estimate=cost(0, 2 * count * plan.slots),
        compiler_params=PARAMS,
        name="far_picks",
    )(on_chip(routes), after)


def far_gates_body(plan, routes_ref, gates_ref, after_ref, high_ref, low_ref):
    first, second = slot_rows(routes_ref[...], plan.experts, plan.cap)
    high_ref[...], low_ref[...] = gate_pair(plan, first, second, gates_ref[...])


def spread_gates(plan, routes, gates, after):
    count = routes.shape[1]
    return pl.pallas_call(
        functools.partial(far_gates_body, plan),
        in_specs=[VMEM] * 2 + [ANY],
        out_specs=[VMEM] * 2,
        out_shape=[pltpu.VMEM((count, plan.slots), BF16)] * 2,
        cost_estimate=cost(0, 4 * count * plan.slots),
        compiler_params=PARAMS,
        name="spread_gates",
    )(on_chip(routes), on_chip(gates), after)


def pick_body(plan, pick_ref, tokens_ref, *out_refs):
    tokens = tokens_ref[...]
    for j, out_ref in enumerate(out_refs):
        pick = pick_ref[j * plan.piece_rows : (j + 1) * plan.piece_rows, :]
        out_ref[...] = jnp.dot(pick, tokens, preferred_element_type=F32).astype(BF16)


def pick_rows(plan, pick, chunk):
    width = chunk.shape[1]
    return pl.pallas_call(
        functools.partial(pick_body, plan),
        in_specs=[VMEM] * 2,
        out_specs=[VMEM] * plan.pieces,
        out_shape=[pltpu.VMEM((plan.piece_rows, width), BF16)] * plan.pieces,
        cost_estimate=cost(2 * pick.size * width, 2 * plan.slots * width),
        compiler_params=PARAMS,
        name="pick_rows",
    )(on_chip(pick), on_chip(chunk))


def weigh(high, low, parts):
    return jnp.dot(high, parts, preferred_element_type=F32) + jnp.dot(low, parts, preferred_element_type=F32)


def relay_body(high_ref, low_ref, *refs):
    parts = jnp.concatenate([ref[...] for ref in refs[:-1]], axis=0)
    refs[-1][...] = weigh(high_ref[...], low_ref[...], parts).astype(BF16)


def relay_sum(high, low, parts):
    count, slots = high.shape
    width = parts[0].shape[1]
    return pl.pallas_call(
        relay_body,
        in_specs=[VMEM] * (2 + len(parts)),
        out_specs=VMEM,
        out_shape=pltpu.VMEM((count, width), BF16),
        cost_estimate=cost(4 * count * slots * width, 2 * (slots + count) * width),
        compiler_params=PARAMS,
        name="relay_sum",
    )(on_chip(high), on_chip(low), *[on_chip(part) for part in parts])


def near_sum_body(plan, routes_ref, gates_ref, tokens_ref, after_ref, *refs):
    first, second = slot_rows(routes_ref[...], plan.experts, plan.cap)
    high, low = gate_pair(plan, first, second, gates_ref[...])
    parts = jnp.concatenate([ref[...] for ref in refs[:-1]], axis=0)
    refs[-1][...] = tokens_ref[...].astype(F32) + weigh(high, low, parts)


def near_sum(plan, routes, gates, tokens, parts, after):
    return pl.pallas_call(
        functools.partial(near_sum_body, plan),
        in_specs=[VMEM] * 3 + [ANY] + [VMEM] * len(parts),
        out_specs=VMEM,
        out_shape=pltpu.VMEM(tokens.shape, F32),
        cost_estimate=cost(4 * plan.slots * tokens.size, 10 * tokens.size),
        compiler_params=PARAMS,
        name="near_sum",
    )(routes, gates, tokens, after, *[on_chip(part) for part in parts])


def final_body(base_ref, *refs):
    at = 0
    for ref in refs[:-1]:
        span = slice(at, at + ref.shape[1])
        refs[-1][:, span] = (base_ref[:, span] + ref[...].astype(F32)).astype(BF16)
        at += ref.shape[1]


def final_sum(base, far):
    return pl.pallas_call(
        final_body,
        in_specs=[VMEM] * (1 + len(far)),
        out_specs=VMEM,
        out_shape=jax.ShapeDtypeStruct(base.shape, BF16),
        cost_estimate=cost(2 * base.size, 8 * base.size),
        compiler_params=PARAMS,
        name="final_sum",
    )(on_chip(base), *[on_chip(chunk) for chunk in far])


def hidden_units(rows, w_in, half_units):
    gate = jnp.dot(rows, w_in[0, :, 0:half_units], preferred_element_type=F32)
    up = jnp.dot(rows, w_in[0, :, half_units:], preferred_element_type=F32)
    return (jax.nn.silu(gate) * up).astype(BF16)


def down_sum(hidden, downs, at):
    partials = [jnp.dot(h, down[0, :, at], preferred_element_type=F32) for h, down in zip(hidden, downs)]
    return (partials[0] + partials[1]).astype(BF16)


def expert_body(pieces, *refs):
    parts, refs = refs[:pieces], refs[pieces:]
    (in_a, down_a, in_b, down_b, _), refs = refs[:5], refs[5:]
    outs, (hid_a, hid_b) = refs[:pieces], refs[pieces : pieces + 2]
    size, width = outs[0].shape
    half_units = down_a.shape[1]
    rows = jnp.concatenate([part[...] for part in parts], axis=0)
    hid_a[...] = hidden_units(rows, in_a, half_units)
    hid_b[...] = hidden_units(rows, in_b, half_units)
    total = down_sum((hid_a[...], hid_b[...]), (down_a, down_b), slice(0, width))
    for i, out in enumerate(outs):
        out[...] = total[i * size : (i + 1) * size, :]


def expert(parts, weights, after, width):
    pieces = len(parts)
    size = parts[0].shape[0]
    features, half_units = weights[0].shape[1], weights[1].shape[1]
    slots = pieces * size
    outs = pl.pallas_call(
        functools.partial(expert_body, pieces),
        in_specs=[VMEM] * (pieces + 4) + [ANY],
        out_specs=[VMEM] * (pieces + 2),
        out_shape=[pltpu.VMEM((size, width), BF16)] * pieces + [pltpu.VMEM((slots, half_units), BF16)] * 2,
        cost_estimate=pl.CostEstimate(
            flops=4 * slots * half_units * (2 * features + width),
            transcendentals=2 * slots * half_units,
            bytes_accessed=2 * slots * (features + width),
        ),
        compiler_params=PARAMS,
    )(*[on_chip(part) for part in parts], *weights, after)
    return outs[:pieces], outs[pieces:]


def rest_body(pieces, hid_a, hid_b, down_a, down_b, *outs):
    size = outs[0].shape[0]
    at = down_a.shape[2] - sum(out.shape[1] for out in outs[::pieces])
    for c in range(len(outs) // pieces):
        width = outs[c * pieces].shape[1]
        total = down_sum((hid_a[...], hid_b[...]), (down_a, down_b), slice(at, at + width))
        for i in range(pieces):
            outs[c * pieces + i][...] = total[i * size : (i + 1) * size, :]
        at += width


def expert_rest(hidden, weights, pieces, widths):
    slots, half_units = hidden[0].shape
    size = slots // pieces
    outs = pl.pallas_call(
        functools.partial(rest_body, pieces),
        in_specs=[VMEM] * 4,
        out_specs=[VMEM] * (pieces * len(widths)),
        out_shape=[pltpu.VMEM((size, width), BF16) for width in widths for _ in range(pieces)],
        cost_estimate=cost(4 * slots * half_units * sum(widths), 2 * slots * sum(widths)),
        compiler_params=PARAMS,
        name="far_rest",
    )(*[on_chip(x) for x in hidden], weights[1], weights[3])
    return [outs[c * pieces : (c + 1) * pieces] for c in range(len(widths))]


def local(tokens, routes, gates, w_in, w_down):
    plan = Plan(lax.axis_size("expert"), tokens.shape[0])
    features = tokens.shape[1]
    routes, gates = routes.T, gates.T
    far_routes = plan.across(routes)
    far_tokens = plan.across(tokens)
    far_gates = plan.across(gates)
    partner = [on_chip(plan.partner(w)) for w in (w_in, w_down)]
    near_picked = select(plan, routes, tokens)
    near_rows = plan.near_exchange(near_picked)
    weights = list(stage((w_in, w_down), near_picked[0])) + partner
    pick = far_picks(plan, far_routes, weights[1])
    far_picked = pick_rows(plan, pick, far_tokens)
    far_rows = plan.near_exchange(far_picked)
    near_out, _ = expert(near_rows, weights, far_picked[0], features)
    near_back = plan.near_exchange(near_out)
    high, low = spread_gates(plan, far_routes, far_gates, near_out[0])
    widths = [b - a for a, b in spans(BACK_WIDTHS, features)]
    first_out, hidden = expert(far_rows, weights, high, widths[0])
    far_out = [first_out] + expert_rest(hidden, weights, plan.pieces, widths[1:])
    far_total = []
    for c in range(len(widths)):
        far_back = plan.near_exchange(far_out[c])
        far_sum = relay_sum(high, low, far_back)
        far_total.append(plan.across(far_sum))
    base = near_sum(plan, routes, gates, tokens, near_back, far_sum)
    return final_sum(base, far_total)


def solution(mesh):
    in_specs = (
        P(("groups", "expert"), None),
        P(("groups", "expert"), None),
        P(("groups", "expert"), None),
        P("expert", None, None),
        P("expert", None, None),
    )
    out_specs = P(("groups", "expert"), None)

    return jax.shard_map(local, mesh=mesh, in_specs=in_specs, out_specs=out_specs, check_vma=False)
```

profile of v0, /device:TPU:6, one launch (start us, length us, event | category | flops | bytes accessed | tf_op | source)
XLA Modules:
  0.0 99.9 jit_solution(10477790953718353142)
XLA Ops:
  0.5 2.6 %collective-permute-start.7 = (bf16[256,1024]{1,0:T(8,128)(2,1)}, bf16[256,1024]{1,0:T(8,128)(2,1)S(1)}, u32[]{:S(2)}, u32[]{:S(2)}) collective-permute-start(bf16[256,1024]{1,0:T(8,128)(2,1)} %tokens_ref.3), channel_id=1, source_target_pairs={{0,8},{1,9},{2,10},{3,11},{4,12},{5,13},{6,14},{7,15},{8,0},{9,1},... | collective-permute-start | bytes 1572872 | tf_op jit(solution)/shard_map/ppermute | solution.py:74
  3.4 1.5 %select.1 = (bf16[128,1024]{1,0:T(8,128)(2,1)S(1)}, bf16[128,1024]{1,0:T(8,128)(2,1)S(1)}, bf16[128,1024]{1,0:T(8,128)(2,1)S(1)}, bf16[128,1024]{1,0:T(8,128)(2,1)S(1)}) custom-call(s32[2,256]{1,0:T(2,128)} %bitcast.3, bf16[256,1024]{1,0:T(8,128)(2,1)} %tokens_ref.3), custom_call_target="tpu_custom_call" | custom-call | flops 268435456 | bytes 1048576 | tf_op jit(solution)/shard_map/select/pallas_call | solution.py:160
  5.6 21.2 %collective-permute-done.routes_ref = s32[2,256]{1,0:T(2,128)S(1)} collective-permute-done((s32[2,256]{1,0:T(2,128)}, s32[2,256]{1,0:T(2,128)S(1)}, u32[]{:S(2)}, u32[]{:S(2)}) %collective-permute-start) | collective-permute-done | bytes 2080 | tf_op jit(solution)/shard_map/ppermute | solution.py:74
  26.8 0.8 collective-permute-start.3
  27.5 1.2 %collective-permute-start.4 = (bf16[128,1024]{1,0:T(8,128)(2,1)S(1)}, bf16[128,1024]{1,0:T(8,128)(2,1)S(1)}, u32[]{:S(2)}, u32[]{:S(2)}) collective-permute-start(bf16[128,1024]{1,0:T(8,128)(2,1)S(1)} %get-tuple-element.34), channel_id=1, source_target_pairs={{0,6},{1,7},{2,4},{3,5},{4,2},{5,3},{6,0},{7,1},{8,14},{9,15},{10,... | collective-permute-start | bytes 786440 | tf_op jit(solution)/shard_map/ppermute | solution.py:82
  28.8 2.9 %stage.1 = (bf16[1,1024,2048]{2,1,0:T(8,128)(2,1)S(1)}, bf16[1,1024,1024]{2,1,0:T(8,128)(2,1)S(1)}) custom-call(bf16[1,1024,2048]{2,1,0:T(8,128)(2,1)} %refs_0_.1, bf16[1,1024,1024]{2,1,0:T(8,128)(2,1)} %refs_1_.1, bf16[128,1024]{1,0:T(8,128)(2,1)S(1)} %get-tuple-element.31.refs_2_.refs_0_), custom_call_target="tpu_custom_call" | custom-call | bytes 12582912 | tf_op jit(solution)/shard_map/stage/pallas_call | solution.py:130
  32.4 2.2 %collective-permute-start.1 = (f32[2,256]{1,0:T(2,128)S(1)}, f32[2,256]{1,0:T(2,128)S(1)}, u32[]{:S(2)}, u32[]{:S(2)}) collective-permute-start(f32[2,256]{1,0:T(2,128)S(1)} %bitcast.5), channel_id=1, source_target_pairs={{0,8},{1,9},{2,10},{3,11},{4,12},{5,13},{6,14},{7,15},{8,0},{9,1},... | collective-permute-start | bytes 6152 | tf_op jit(solution)/shard_map/ppermute | solution.py:74
  34.6 1.4 %collective-permute-done.3.refs_2_ = bf16[128,1024]{1,0:T(8,128)(2,1)S(1)} collective-permute-done((bf16[128,1024]{1,0:T(8,128)(2,1)S(1)}, bf16[128,1024]{1,0:T(8,128)(2,1)S(1)}, u32[]{:S(2)}, u32[]{:S(2)}) %collective-permute-start.3) | collective-permute-done | bytes 262176 | tf_op jit(solution)/shard_map/ppermute | solution.py:82
  36.0 1.6 %collective-permute-start.10 = (bf16[128,1024]{1,0:T(8,128)(2,1)S(1)}, bf16[128,1024]{1,0:T(8,128)(2,1)S(1)}, u32[]{:S(2)}, u32[]{:S(2)}) collective-permute-start(bf16[128,1024]{1,0:T(8,128)(2,1)S(1)} %get-tuple-element.43), channel_id=1, source_target_pairs={{0,6},{1,7},{2,4},{3,5},{4,2},{5,3},{6,0},{7,1},{8,14},{9,15},{10,... | collective-permute-start | bytes 786440 | tf_op jit(solution)/shard_map/ppermute | solution.py:82
  37.5 4.1 %collective-permute-done.4.refs_3_ = bf16[128,1024]{1,0:T(8,128)(2,1)S(1)} collective-permute-done((bf16[128,1024]{1,0:T(8,128)(2,1)S(1)}, bf16[128,1024]{1,0:T(8,128)(2,1)S(1)}, u32[]{:S(2)}, u32[]{:S(2)}) %collective-permute-start.4) | collective-permute-done | bytes 262176 | tf_op jit(solution)/shard_map/ppermute | solution.py:82
  41.7 1.5 %collective-permute-start.8 = (bf16[128,1024]{1,0:T(8,128)(2,1)S(1)}, bf16[128,1024]{1,0:T(8,128)(2,1)S(1)}, u32[]{:S(2)}, u32[]{:S(2)}) collective-permute-start(bf16[128,1024]{1,0:T(8,128)(2,1)S(1)} %get-tuple-element.41), channel_id=1, source_target_pairs={{0,2},{1,3},{2,0},{3,1},{4,6},{5,7},{6,4},{7,5},{8,10},{9,11},{10,... | collective-permute-start | bytes 786440 | tf_op jit(solution)/shard_map/ppermute | solution.py:82
  43.2 0.6 collective-permute-start.9
  43.8 7.7 %shard_map.55 = (bf16[128,1024]{1,0:T(8,128)(2,1)S(1)}, bf16[128,1024]{1,0:T(8,128)(2,1)S(1)}, bf16[128,1024]{1,0:T(8,128)(2,1)S(1)}, bf16[128,1024]{1,0:T(8,128...) custom-call(bf16[128,1024]{1,0:T(8,128)(2,1)S(1)} %get-tuple-element.31.refs_2_.refs_0_, ...), custom_call_target="tpu_custom_call" | custom-call | flops 6442450944 | bytes 2097152 | tf_op jit(solution)/shard_map/pallas_call | solution.py:324
  51.5 0.8 spread_gates.1
  52.3 5.6 %shard_map.56 = (bf16[128,512]{1,0:T(8,128)(2,1)S(1)}, bf16[128,512]{1,0:T(8,128)(2,1)S(1)}, bf16[128,512]{1,0:T(8,128)(2,1)S(1)}, bf16[128,512]{1,0:T(8,128)(2,...) custom-call(bf16[128,1024]{1,0:T(8,128)(2,1)S(1)} %get-tuple-element.37.refs_8_.refs_0_, ...), custom_call_target="tpu_custom_call" | custom-call | flops 5368709120 | bytes 1572864 | tf_op jit(solution)/shard_map/pallas_call | solution.py:324
  58.5 1.4 %collective-permute-start.18 = (bf16[128,512]{1,0:T(8,128)(2,1)S(1)}, bf16[128,512]{1,0:T(8,128)(2,1)S(1)}, u32[]{:S(2)}, u32[]{:S(2)}) collective-permute-start(bf16[128,512]{1,0:T(8,128)(2,1)S(1)} %get-tuple-element.55), channel_id=1, source_target_pairs={{0,4},{1,5},{2,6},{3,7},{4,0},{5,1},{6,2},{7,3},{8,12},{9,13},{10,... | collective-permute-start | bytes 393224 | tf_op jit(solution)/shard_map/ppermute | solution.py:82
  59.9 1.6 %collective-permute-start.19 = (bf16[128,512]{1,0:T(8,128)(2,1)S(1)}, bf16[128,512]{1,0:T(8,128)(2,1)S(1)}, u32[]{:S(2)}, u32[]{:S(2)}) collective-permute-start(bf16[128,512]{1,0:T(8,128)(2,1)S(1)} %get-tuple-element.56), channel_id=1, source_target_pairs={{0,6},{1,7},{2,4},{3,5},{4,2},{5,3},{6,0},{7,1},{8,14},{9,15},{10,... | collective-permute-start | bytes 393224 | tf_op jit(solution)/shard_map/ppermute | solution.py:82
  61.5 1.4 %far_rest.1 = (bf16[128,512]{1,0:T(8,128)(2,1)S(1)}, bf16[128,512]{1,0:T(8,128)(2,1)S(1)}, bf16[128,512]{1,0:T(8,128)(2,1)S(1)}, bf16[128,512]{1,0:T(8,128)(2,1)S(1)}) custom-call(bf16[512,1024]{1,0:T(8,128)(2,1)S(1)} %get-tuple-element.44.hid_a, bf16[512,1024]{1,0:T(8,128)(2,1)S(1)} %get-tuple-element.45.hid_b, ...), custom_call_target="tpu_custom_call" | custom-call | flops 1073741824 | bytes 524288 | tf_op jit(solution)/shard_map/far_rest/pallas_call | solution.py:353
  63.4 1.4 %collective-permute-start.12 = (bf16[128,512]{1,0:T(8,128)(2,1)S(1)}, bf16[128,512]{1,0:T(8,128)(2,1)S(1)}, u32[]{:S(2)}, u32[]{:S(2)}) collective-permute-start(bf16[128,512]{1,0:T(8,128)(2,1)S(1)} %get-tuple-element.48), channel_id=1, source_target_pairs={{0,4},{1,5},{2,6},{3,7},{4,0},{5,1},{6,2},{7,3},{8,12},{9,13},{10,... | collective-permute-start | bytes 393224 | tf_op jit(solution)/shard_map/ppermute | solution.py:82
  64.9 1.6 %collective-permute-start.13 = (bf16[128,512]{1,0:T(8,128)(2,1)S(1)}, bf16[128,512]{1,0:T(8,128)(2,1)S(1)}, u32[]{:S(2)}, u32[]{:S(2)}) collective-permute-start(bf16[128,512]{1,0:T(8,128)(2,1)S(1)} %get-tuple-element.49), channel_id=1, source_target_pairs={{0,6},{1,7},{2,4},{3,5},{4,2},{5,3},{6,0},{7,1},{8,14},{9,15},{10,... | collective-permute-start | bytes 393224 | tf_op jit(solution)/shard_map/ppermute | solution.py:82
  66.4 1.3 %collective-permute-start.14 = (bf16[128,1024]{1,0:T(8,128)(2,1)S(1)}, bf16[128,1024]{1,0:T(8,128)(2,1)S(1)}, u32[]{:S(2)}, u32[]{:S(2)}) collective-permute-start(bf16[128,1024]{1,0:T(8,128)(2,1)S(1)} %get-tuple-element.50), channel_id=1, source_target_pairs={{0,2},{1,3},{2,0},{3,1},{4,6},{5,7},{6,4},{7,5},{8,10},{9,11},{10,... | collective-permute-start | bytes 786440 | tf_op jit(solution)/shard_map/ppermute | solution.py:82
  67.8 0.9 collective-permute-done.19.refs_3_
  68.7 0.6 collective-permute-start.15
  69.3 2.8 %collective-permute-done.11.refs_1_ = bf16[128,512]{1,0:T(8,128)(2,1)S(1)} collective-permute-done((bf16[128,512]{1,0:T(8,128)(2,1)S(1)}, bf16[128,512]{1,0:T(8,128)(2,1)S(1)}, u32[]{:S(2)}, u32[]{:S(2)}) %collective-permute-start.11) | collective-permute-done | bytes 131104 | tf_op jit(solution)/shard_map/ppermute | solution.py:82
  72.1 1.4 %collective-permute-start.16 = (bf16[128,1024]{1,0:T(8,128)(2,1)S(1)}, bf16[128,1024]{1,0:T(8,128)(2,1)S(1)}, u32[]{:S(2)}, u32[]{:S(2)}) collective-permute-start(bf16[128,1024]{1,0:T(8,128)(2,1)S(1)} %get-tuple-element.52), channel_id=1, source_target_pairs={{0,6},{1,7},{2,4},{3,5},{4,2},{5,3},{6,0},{7,1},{8,14},{9,15},{10,... | collective-permute-start | bytes 786440 | tf_op jit(solution)/shard_map/ppermute | solution.py:82
  73.9 3.3 %collective-permute-start.20 = (bf16[256,512]{1,0:T(8,128)(2,1)S(1)}, bf16[256,512]{1,0:T(8,128)(2,1)S(1)}, u32[]{:S(2)}, u32[]{:S(2)}) collective-permute-start(bf16[256,512]{1,0:T(8,128)(2,1)S(1)} %relay_sum.3), channel_id=1, source_target_pairs={{0,8},{1,9},{2,10},{3,11},{4,12},{5,13},{6,14},{7,15},{8,0},{9,1},... | collective-permute-start | bytes 786440 | tf_op jit(solution)/shard_map/ppermute | solution.py:74
  77.6 6.7 %collective-permute-start.21 = (bf16[256,512]{1,0:T(8,128)(2,1)S(1)}, bf16[256,512]{1,0:T(8,128)(2,1)S(1)}, u32[]{:S(2)}, u32[]{:S(2)}) collective-permute-start(bf16[256,512]{1,0:T(8,128)(2,1)S(1)} %relay_sum.2.after_ref), channel_id=1, source_target_pairs={{0,8},{1,9},{2,10},{3,11},{4,12},{5,13},{6,14},{7,15},{8,0},{9,1},... | collective-permute-start | bytes 786440 | tf_op jit(solution)/shard_map/ppermute | solution.py:74
  84.3 3.5 %collective-permute-done.15.refs_2_ = bf16[128,1024]{1,0:T(8,128)(2,1)S(1)} collective-permute-done((bf16[128,1024]{1,0:T(8,128)(2,1)S(1)}, bf16[128,1024]{1,0:T(8,128)(2,1)S(1)}, u32[]{:S(2)}, u32[]{:S(2)}) %collective-permute-start.15) | collective-permute-done | bytes 262176 | tf_op jit(solution)/shard_map/ppermute | solution.py:82
  87.8 7.2 %collective-permute-done.16.refs_3_ = bf16[128,1024]{1,0:T(8,128)(2,1)S(1)} collective-permute-done((bf16[128,1024]{1,0:T(8,128)(2,1)S(1)}, bf16[128,1024]{1,0:T(8,128)(2,1)S(1)}, u32[]{:S(2)}, u32[]{:S(2)}) %collective-permute-start.16) | collective-permute-done | bytes 262176 | tf_op jit(solution)/shard_map/ppermute | solution.py:82
  95.0 1.5 %near_sum.1.base_ref = f32[256,1024]{1,0:T(8,128)S(1)} custom-call(s32[2,256]{1,0:T(2,128)S(1)} %bitcast.4, f32[2,256]{1,0:T(2,128)S(1)} %bitcast.6, bf16[256,1024]{1,0:T(8,128)(2,1)S(1)} %copy-done, bf16[256,512]{1,0:T(8,128)(2,1)S(1)} %relay_sum.2.after_ref, bf16[128,1024]{1,0:T(8,128)(2,1)S(1)} %get-tuple-element.38.after_ref.refs_0_, ...), custom_call_target="tpu_custom_call" | custom-call | flops 536870912 | bytes 2621440 | tf_op jit(solution)/shard_map/near_sum/pallas_call | solution.py:263
  96.5 2.5 %collective-permute-done.21.refs_1_ = bf16[256,512]{1,0:T(8,128)(2,1)S(1)} collective-permute-done((bf16[256,512]{1,0:T(8,128)(2,1)S(1)}, bf16[256,512]{1,0:T(8,128)(2,1)S(1)}, u32[]{:S(2)}, u32[]{:S(2)}) %collective-permute-start.21) | collective-permute-done | bytes 262176 | tf_op jit(solution)/shard_map/ppermute | solution.py:74
  99.0 0.9 final_sum.1
  (30 shorter events, 4.2 us)
Async XLA Ops:
  0.0 43.8 %collective-permute-start.5 = (bf16[1,1024,2048]{2,1,0:T(8,128)(2,1)}, bf16[1,1024,2048]{2,1,0:T(8,128)(2,1)S(1)}, u32[]{:S(2)}, u32[]{:S(2)}) collective-permute-start(bf16[1,1024,2048]{2,1,0:T(8,128)(2,1)} %refs_0_.1), channel_id=1, source_target_pairs={{0,1},{1,0},{2,3},{3,2},{4,5},{5,4},{6,7},{7,6},{8,9},{9,8},{10,11... | collective-permute-start | bytes 12582920 | tf_op jit(solution)/shard_map/ppermute | solution.py:77
  0.0 43.2 %collective-permute-start.6 = (bf16[1,1024,1024]{2,1,0:T(8,128)(2,1)}, bf16[1,1024,1024]{2,1,0:T(8,128)(2,1)S(1)}, u32[]{:S(2)}, u32[]{:S(2)}) collective-permute-start(bf16[1,1024,1024]{2,1,0:T(8,128)(2,1)} %refs_1_.1), channel_id=1, source_target_pairs={{0,1},{1,0},{2,3},{3,2},{4,5},{5,4},{6,7},{7,6},{8,9},{9,8},{10,11... | collective-permute-start | bytes 6291464 | tf_op jit(solution)/shard_map/ppermute | solution.py:77
  0.5 27.0 %collective-permute-start.7 = (bf16[256,1024]{1,0:T(8,128)(2,1)}, bf16[256,1024]{1,0:T(8,128)(2,1)S(1)}, u32[]{:S(2)}, u32[]{:S(2)}) collective-permute-start(bf16[256,1024]{1,0:T(8,128)(2,1)} %tokens_ref.3), channel_id=1, source_target_pairs={{0,8},{1,9},{2,10},{3,11},{4,12},{5,13},{6,14},{7,15},{8,0},{9,1},... | collective-permute-start | bytes 1572872 | tf_op jit(solution)/shard_map/ppermute | solution.py:74
  3.1 23.7 %collective-permute-start = (s32[2,256]{1,0:T(2,128)}, s32[2,256]{1,0:T(2,128)S(1)}, u32[]{:S(2)}, u32[]{:S(2)}) collective-permute-start(s32[2,256]{1,0:T(2,128)} %bitcast.2), channel_id=1, source_target_pairs={{0,8},{1,9},{2,10},{3,11},{4,12},{5,13},{6,14},{7,15},{8,0},{9,1},... | collective-permute-start | bytes 6152 | tf_op jit(solution)/shard_map/ppermute | solution.py:74
  5.0 27.4 %collective-permute-start.2 = (bf16[128,1024]{1,0:T(8,128)(2,1)S(1)}, bf16[128,1024]{1,0:T(8,128)(2,1)S(1)}, u32[]{:S(2)}, u32[]{:S(2)}) collective-permute-start(bf16[128,1024]{1,0:T(8,128)(2,1)S(1)} %get-tuple-element.32), channel_id=1, source_target_pairs={{0,2},{1,3},{2,0},{3,1},{4,6},{5,7},{6,4},{7,5},{8,10},{9,11},{10,... | collective-permute-start | bytes 786440 | tf_op jit(solution)/shard_map/ppermute | solution.py:82
  26.8 9.2 %collective-permute-start.3 = (bf16[128,1024]{1,0:T(8,128)(2,1)S(1)}, bf16[128,1024]{1,0:T(8,128)(2,1)S(1)}, u32[]{:S(2)}, u32[]{:S(2)}) collective-permute-start(bf16[128,1024]{1,0:T(8,128)(2,1)S(1)} %get-tuple-element.33), channel_id=1, source_target_pairs={{0,4},{1,5},{2,6},{3,7},{4,0},{5,1},{6,2},{7,3},{8,12},{9,13},{10,... | collective-permute-start | bytes 786440 | tf_op jit(solution)/shard_map/ppermute | solution.py:82
  27.5 14.1 %collective-permute-start.4 = (bf16[128,1024]{1,0:T(8,128)(2,1)S(1)}, bf16[128,1024]{1,0:T(8,128)(2,1)S(1)}, u32[]{:S(2)}, u32[]{:S(2)}) collective-permute-start(bf16[128,1024]{1,0:T(8,128)(2,1)S(1)} %get-tuple-element.34), channel_id=1, source_target_pairs={{0,6},{1,7},{2,4},{3,5},{4,2},{5,3},{6,0},{7,1},{8,14},{9,15},{10,... | collective-permute-start | bytes 786440 | tf_op jit(solution)/shard_map/ppermute | solution.py:82
  28.8 3.7 %copy-start.2 = (f32[256,2]{0,1:T(2,128)S(1)}, f32[256,2]{0,1:T(2,128)}, u32[]{:S(2)}) copy-start(f32[256,2]{0,1:T(2,128)} %param.7) | copy-start | bytes 6148
  32.4 19.0 %collective-permute-start.1 = (f32[2,256]{1,0:T(2,128)S(1)}, f32[2,256]{1,0:T(2,128)S(1)}, u32[]{:S(2)}, u32[]{:S(2)}) collective-permute-start(f32[2,256]{1,0:T(2,128)S(1)} %bitcast.5), channel_id=1, source_target_pairs={{0,8},{1,9},{2,10},{3,11},{4,12},{5,13},{6,14},{7,15},{8,0},{9,1},... | collective-permute-start | bytes 6152 | tf_op jit(solution)/shard_map/ppermute | solution.py:74
  36.0 16.3 %collective-permute-start.10 = (bf16[128,1024]{1,0:T(8,128)(2,1)S(1)}, bf16[128,1024]{1,0:T(8,128)(2,1)S(1)}, u32[]{:S(2)}, u32[]{:S(2)}) collective-permute-start(bf16[128,1024]{1,0:T(8,128)(2,1)S(1)} %get-tuple-element.43), channel_id=1, source_target_pairs={{0,6},{1,7},{2,4},{3,5},{4,2},{5,3},{6,0},{7,1},{8,14},{9,15},{10,... | collective-permute-start | bytes 786440 | tf_op jit(solution)/shard_map/ppermute | solution.py:82
  41.7 10.6 %collective-permute-start.8 = (bf16[128,1024]{1,0:T(8,128)(2,1)S(1)}, bf16[128,1024]{1,0:T(8,128)(2,1)S(1)}, u32[]{:S(2)}, u32[]{:S(2)}) collective-permute-start(bf16[128,1024]{1,0:T(8,128)(2,1)S(1)} %get-tuple-element.41), channel_id=1, source_target_pairs={{0,2},{1,3},{2,0},{3,1},{4,6},{5,7},{6,4},{7,5},{8,10},{9,11},{10,... | collective-permute-start | bytes 786440 | tf_op jit(solution)/shard_map/ppermute | solution.py:82
  43.2 9.1 %collective-permute-start.9 = (bf16[128,1024]{1,0:T(8,128)(2,1)S(1)}, bf16[128,1024]{1,0:T(8,128)(2,1)S(1)}, u32[]{:S(2)}, u32[]{:S(2)}) collective-permute-start(bf16[128,1024]{1,0:T(8,128)(2,1)S(1)} %get-tuple-element.42), channel_id=1, source_target_pairs={{0,4},{1,5},{2,6},{3,7},{4,0},{5,1},{6,2},{7,3},{8,12},{9,13},{10,... | collective-permute-start | bytes 786440 | tf_op jit(solution)/shard_map/ppermute | solution.py:82
  57.9 7.0 %collective-permute-start.17 = (bf16[128,512]{1,0:T(8,128)(2,1)S(1)}, bf16[128,512]{1,0:T(8,128)(2,1)S(1)}, u32[]{:S(2)}, u32[]{:S(2)}) collective-permute-start(bf16[128,512]{1,0:T(8,128)(2,1)S(1)} %get-tuple-element.54), channel_id=1, source_target_pairs={{0,2},{1,3},{2,0},{3,1},{4,6},{5,7},{6,4},{7,5},{8,10},{9,11},{10,... | collective-permute-start | bytes 393224 | tf_op jit(solution)/shard_map/ppermute | solution.py:82
  58.5 8.0 %collective-permute-start.18 = (bf16[128,512]{1,0:T(8,128)(2,1)S(1)}, bf16[128,512]{1,0:T(8,128)(2,1)S(1)}, u32[]{:S(2)}, u32[]{:S(2)}) collective-permute-start(bf16[128,512]{1,0:T(8,128)(2,1)S(1)} %get-tuple-element.55), channel_id=1, source_target_pairs={{0,4},{1,5},{2,6},{3,7},{4,0},{5,1},{6,2},{7,3},{8,12},{9,13},{10,... | collective-permute-start | bytes 393224 | tf_op jit(solution)/shard_map/ppermute | solution.py:82
  59.9 8.8 %collective-permute-start.19 = (bf16[128,512]{1,0:T(8,128)(2,1)S(1)}, bf16[128,512]{1,0:T(8,128)(2,1)S(1)}, u32[]{:S(2)}, u32[]{:S(2)}) collective-permute-start(bf16[128,512]{1,0:T(8,128)(2,1)S(1)} %get-tuple-element.56), channel_id=1, source_target_pairs={{0,6},{1,7},{2,4},{3,5},{4,2},{5,3},{6,0},{7,1},{8,14},{9,15},{10,... | collective-permute-start | bytes 393224 | tf_op jit(solution)/shard_map/ppermute | solution.py:82
  61.4 33.6 %copy-start = (bf16[256,1024]{1,0:T(8,128)(2,1)S(1)}, bf16[256,1024]{1,0:T(8,128)(2,1)}, u32[]{:S(2)}) copy-start(bf16[256,1024]{1,0:T(8,128)(2,1)} %tokens_ref.3) | copy-start | bytes 1572868
  61.4 33.6 %copy-start.1 = (s32[256,2]{0,1:T(2,128)S(1)}, s32[256,2]{0,1:T(2,128)}, u32[]{:S(2)}) copy-start(s32[256,2]{0,1:T(2,128)} %param.6) | copy-start | bytes 6148
  62.9 9.2 %collective-permute-start.11 = (bf16[128,512]{1,0:T(8,128)(2,1)S(1)}, bf16[128,512]{1,0:T(8,128)(2,1)S(1)}, u32[]{:S(2)}, u32[]{:S(2)}) collective-permute-start(bf16[128,512]{1,0:T(8,128)(2,1)S(1)} %get-tuple-element.47), channel_id=1, source_target_pairs={{0,2},{1,3},{2,0},{3,1},{4,6},{5,7},{6,4},{7,5},{8,10},{9,11},{10,... | collective-permute-start | bytes 393224 | tf_op jit(solution)/shard_map/ppermute | solution.py:82
  63.4 10.5 %collective-permute-start.12 = (bf16[128,512]{1,0:T(8,128)(2,1)S(1)}, bf16[128,512]{1,0:T(8,128)(2,1)S(1)}, u32[]{:S(2)}, u32[]{:S(2)}) collective-permute-start(bf16[128,512]{1,0:T(8,128)(2,1)S(1)} %get-tuple-element.48), channel_id=1, source_target_pairs={{0,4},{1,5},{2,6},{3,7},{4,0},{5,1},{6,2},{7,3},{8,12},{9,13},{10,... | collective-permute-start | bytes 393224 | tf_op jit(solution)/shard_map/ppermute | solution.py:82
  64.9 12.3 %collective-permute-start.13 = (bf16[128,512]{1,0:T(8,128)(2,1)S(1)}, bf16[128,512]{1,0:T(8,128)(2,1)S(1)}, u32[]{:S(2)}, u32[]{:S(2)}) collective-permute-start(bf16[128,512]{1,0:T(8,128)(2,1)S(1)} %get-tuple-element.49), channel_id=1, source_target_pairs={{0,6},{1,7},{2,4},{3,5},{4,2},{5,3},{6,0},{7,1},{8,14},{9,15},{10,... | collective-permute-start | bytes 393224 | tf_op jit(solution)/shard_map/ppermute | solution.py:82
  66.4 17.9 %collective-permute-start.14 = (bf16[128,1024]{1,0:T(8,128)(2,1)S(1)}, bf16[128,1024]{1,0:T(8,128)(2,1)S(1)}, u32[]{:S(2)}, u32[]{:S(2)}) collective-permute-start(bf16[128,1024]{1,0:T(8,128)(2,1)S(1)} %get-tuple-element.50), channel_id=1, source_target_pairs={{0,2},{1,3},{2,0},{3,1},{4,6},{5,7},{6,4},{7,5},{8,10},{9,11},{10,... | collective-permute-start | bytes 786440 | tf_op jit(solution)/shard_map/ppermute | solution.py:82
  68.7 19.1 %collective-permute-start.15 = (bf16[128,1024]{1,0:T(8,128)(2,1)S(1)}, bf16[128,1024]{1,0:T(8,128)(2,1)S(1)}, u32[]{:S(2)}, u32[]{:S(2)}) collective-permute-start(bf16[128,1024]{1,0:T(8,128)(2,1)S(1)} %get-tuple-element.51), channel_id=1, source_target_pairs={{0,4},{1,5},{2,6},{3,7},{4,0},{5,1},{6,2},{7,3},{8,12},{9,13},{10,... | collective-permute-start | bytes 786440 | tf_op jit(solution)/shard_map/ppermute | solution.py:82
  72.1 22.9 %collective-permute-start.16 = (bf16[128,1024]{1,0:T(8,128)(2,1)S(1)}, bf16[128,1024]{1,0:T(8,128)(2,1)S(1)}, u32[]{:S(2)}, u32[]{:S(2)}) collective-permute-start(bf16[128,1024]{1,0:T(8,128)(2,1)S(1)} %get-tuple-element.52), channel_id=1, source_target_pairs={{0,6},{1,7},{2,4},{3,5},{4,2},{5,3},{6,0},{7,1},{8,14},{9,15},{10,... | collective-permute-start | bytes 786440 | tf_op jit(solution)/shard_map/ppermute | solution.py:82
  73.9 22.6 %collective-permute-start.20 = (bf16[256,512]{1,0:T(8,128)(2,1)S(1)}, bf16[256,512]{1,0:T(8,128)(2,1)S(1)}, u32[]{:S(2)}, u32[]{:S(2)}) collective-permute-start(bf16[256,512]{1,0:T(8,128)(2,1)S(1)} %relay_sum.3), channel_id=1, source_target_pairs={{0,8},{1,9},{2,10},{3,11},{4,12},{5,13},{6,14},{7,15},{8,0},{9,1},... | collective-permute-start | bytes 786440 | tf_op jit(solution)/shard_map/ppermute | solution.py:74
  77.6 21.4 %collective-permute-start.21 = (bf16[256,512]{1,0:T(8,128)(2,1)S(1)}, bf16[256,512]{1,0:T(8,128)(2,1)S(1)}, u32[]{:S(2)}, u32[]{:S(2)}) collective-permute-start(bf16[256,512]{1,0:T(8,128)(2,1)S(1)} %relay_sum.2.after_ref), channel_id=1, source_target_pairs={{0,8},{1,9},{2,10},{3,11},{4,12},{5,13},{6,14},{7,15},{8,0},{9,1},... | collective-permute-start | bytes 786440 | tf_op jit(solution)/shard_map/ppermute | solution.py:74
where the time goes:
time: 100 us; the launch traced here: 99.9 us
  waiting for transfers between devices  43.7 us (44%)
  starting transfers between devices  32.2 us (32%)
  Pallas kernels  23.9 us (24%)
    ppermute x5, waiting for transfers between devices, across(): lax.ppermute(x, 'expert', [(i, i ^ self.devices // 2) for i in range(self...  23.7 us
    ppermute x15, waiting for transfers between devices, near_exchange(): lax.ppermute(parts[j], 'expert', [(i, i ^ 2 * j) for i in range(self.devi...  19.9 us
    ppermute x15, starting transfers between devices, near_exchange(): lax.ppermute(parts[j], 'expert', [(i, i ^ 2 * j) for i in range(self.devi...  16.6 us
    ppermute x5, starting transfers between devices, across(): lax.ppermute(x, 'expert', [(i, i ^ self.devices // 2) for i in range(self...  15.1 us
    pallas_call x2, Pallas kernels, expert(): pl.pallas_call(functools.partial(expert_body, pieces), in_specs=[VMEM] *...  13.3 us
    pallas_call x1, Pallas kernels, stage(): pl.pallas_call(functools.partial(stage_body, len(arrays)), in_specs=[HBM]...  2.89 us
  transfers between devices with their start and end apart: 22, of which 8 were waited for; matrix products, arithmetic and copies ran while one was open for 0% of the time, Pallas kernels for 17%

commit v1 on v0

--- a/solution.py
+++ b/solution.py
@@ -10,6 +10,7 @@
 F32 = jnp.float32
 BF16 = jnp.bfloat16
 BACK_WIDTHS = (4, 4)
+DOWN_BLOCK = 512
 ANY = pl.BlockSpec(memory_space=pl.ANY)
 HBM = pl.BlockSpec(memory_space=pltpu.HBM)
 VMEM = pl.BlockSpec(memory_space=pltpu.VMEM)
@@ -78,10 +79,10 @@
 
     def near_exchange(self, parts):
         if self.direct:
-            return [parts[0]] + [
-                lax.ppermute(parts[j], "expert", [(i, i ^ 2 * j) for i in range(self.devices)])
-                for j in range(1, self.pieces)
-            ]
+            got = [parts[0]]
+            for j in range(1, self.pieces):
+                got.append(lax.ppermute(parts[j], "expert", [(i, i ^ 2 * j) for i in range(self.devices)]))
+            return got
         groups = [
             [2 * (half * self.near + chip) + core for chip in range(self.near)]
             for half in range(2)
@@ -302,38 +303,46 @@
     return (partials[0] + partials[1]).astype(BF16)
 
 
-def expert_body(pieces, *refs):
+def expert_body(pieces, chunks, *refs):
     parts, refs = refs[:pieces], refs[pieces:]
     (in_a, down_a, in_b, down_b, _), refs = refs[:5], refs[5:]
-    outs, (hid_a, hid_b) = refs[:pieces], refs[pieces : pieces + 2]
-    size, width = outs[0].shape
+    outs, (hid_a, hid_b) = refs[: chunks * pieces], refs[chunks * pieces :]
+    size = outs[0].shape[0]
     half_units = down_a.shape[1]
     rows = jnp.concatenate([part[...] for part in parts], axis=0)
     hid_a[...] = hidden_units(rows, in_a, half_units)
     hid_b[...] = hidden_units(rows, in_b, half_units)
-    total = down_sum((hid_a[...], hid_b[...]), (down_a, down_b), slice(0, width))
-    for i, out in enumerate(outs):
-        out[...] = total[i * size : (i + 1) * size, :]
-
-
-def expert(parts, weights, after, width):
-    pieces = len(parts)
+    at = 0
+    for c in range(chunks):
+        width = outs[c * pieces].shape[1]
+        step = min(width, DOWN_BLOCK)
+        for low in range(0, width, step):
+            total = down_sum((hid_a[...], hid_b[...]), (down_a, down_b), slice(at + low, at + low + step))
+            for i in range(pieces):
+                outs[c * pieces + i][:, low : low + step] = total[i * size : (i + 1) * size, :]
+        at += width
+
+
+def expert(parts, weights, after, widths, keep=False):
+    pieces, chunks = len(parts), len(widths)
     size = parts[0].shape[0]
     features, half_units = weights[0].shape[1], weights[1].shape[1]
     slots = pieces * size
+    hidden = [pltpu.VMEM((slots, half_units), BF16)] * 2
     outs = pl.pallas_call(
-        functools.partial(expert_body, pieces),
+        functools.partial(expert_body, pieces, chunks),
         in_specs=[VMEM] * (pieces + 4) + [ANY],
-        out_specs=[VMEM] * (pieces + 2),
-        out_shape=[pltpu.VMEM((size, width), BF16)] * pieces + [pltpu.VMEM((slots, half_units), BF16)] * 2,
+        out_specs=[VMEM] * (pieces * chunks + (2 if keep else 0)),
+        out_shape=[pltpu.VMEM((size, width), BF16) for width in widths for _ in range(pieces)] + (hidden if keep else []),
+        scratch_shapes=[] if keep else hidden,
         cost_estimate=pl.CostEstimate(
-            flops=4 * slots * half_units * (2 * features + width),
+            flops=4 * slots * half_units * (2 * features + sum(widths)),
             transcendentals=2 * slots * half_units,
-            bytes_accessed=2 * slots * (features + width),
+            bytes_accessed=2 * slots * (features + sum(widths)),
         ),
         compiler_params=PARAMS,
     )(*[on_chip(part) for part in parts], *weights, after)
-    return outs[:pieces], outs[pieces:]
+    return [outs[c * pieces : (c + 1) * pieces] for c in range(chunks)], outs[chunks * pieces :]
 
 
 def rest_body(pieces, hid_a, hid_b, down_a, down_b, *outs):
@@ -373,18 +382,27 @@
     near_picked = select(plan, routes, tokens)
     near_rows = plan.near_exchange(near_picked)
     weights = list(stage((w_in, w_down), near_picked[0])) + partner
-    pick = far_picks(plan, far_routes, weights[1])
+    widths = [b - a for a, b in spans(BACK_WIDTHS, features)]
+    early = plan.pieces // 2
+    near_early, after = [], weights[1]
+    if early:
+        (near_early,), _ = expert(near_rows[:early], weights, after, (features,))
+        after = near_early[0]
+    pick = far_picks(plan, far_routes, after)
     far_picked = pick_rows(plan, pick, far_tokens)
     far_rows = plan.near_exchange(far_picked)
-    near_out, _ = expert(near_rows, weights, far_picked[0], features)
-    near_back = plan.near_exchange(near_out)
-    high, low = spread_gates(plan, far_routes, far_gates, near_out[0])
-    widths = [b - a for a, b in spans(BACK_WIDTHS, features)]
-    first_out, hidden = expert(far_rows, weights, high, widths[0])
-    far_out = [first_out] + expert_rest(hidden, weights, plan.pieces, widths[1:])
+    (near_late,), _ = expert(near_rows[early:], weights, far_picked[0], (features,))
+    near_back = plan.near_exchange(list(near_early) + list(near_late))
+    far_early, after = [[] for _ in widths], near_late[0]
+    if early:
+        far_early, _ = expert(far_rows[:early], weights, after, widths)
+        after = far_early[0][0]
+    (first_out,), hidden = expert(far_rows[early:], weights, after, widths[:1], keep=True)
+    high, low = spread_gates(plan, far_routes, far_gates, first_out[0])
+    far_late = [first_out] + expert_rest(hidden, weights, plan.pieces - early, widths[1:])
     far_total = []
     for c in range(len(widths)):
-        far_back = plan.near_exchange(far_out[c])
+        far_back = plan.near_exchange(list(far_early[c]) + list(far_late[c]))
         far_sum = relay_sum(high, low, far_back)
         far_total.append(plan.across(far_sum))
     base = near_sum(plan, routes, gates, tokens, near_back, far_sum)

time: 100 us -> 94.1 us (0.941)
  the two profiles are of different devices: /device:TPU:6 before, /device:TPU:0 now
where the time goes in v1:
time: 94.1 us; the launch traced here: 94 us
  waiting for transfers between devices  35.9 us (38%)
  starting transfers between devices  34.8 us (37%)
  Pallas kernels  23.1 us (25%)
    ppermute x15, starting transfers between devices, near_exchange(): lax.ppermute(parts[j], 'expert', [(i, i ^ 2 * j) for i in range(self.devi...  21.9 us
    ppermute x5, waiting for transfers between devices, across(): lax.ppermute(x, 'expert', [(i, i ^ self.devices // 2) for i in range(self...  19.5 us
    ppermute x15, waiting for transfers between devices, near_exchange(): lax.ppermute(parts[j], 'expert', [(i, i ^ 2 * j) for i in range(self.devi...  16.3 us
    pallas_call x4, Pallas kernels, expert(): pl.pallas_call(functools.partial(expert_body, pieces, chunks), in_specs=[...  13.2 us
    ppermute x5, starting transfers between devices, across(): lax.ppermute(x, 'expert', [(i, i ^ self.devices // 2) for i in range(self...  12.4 us
    pallas_call x1, Pallas kernels, stage(): pl.pallas_call(functools.partial(stage_body, len(arrays)), in_specs=[HBM]...  2.88 us
  transfers between devices with their start and end apart: 22, of which 9 were waited for; matrix products, arithmetic and copies ran while one was open for 0% of the time, Pallas kernels for 21%

profile of v1, /device:TPU:0, one launch (start us, length us, event | category | flops | bytes accessed | tf_op | source)
XLA Modules:
  0.0 94.0 jit_solution(3232020905244079465)
XLA Ops:
  0.5 1.5 %select.1 = (bf16[128,1024]{1,0:T(8,128)(2,1)S(1)}, bf16[128,1024]{1,0:T(8,128)(2,1)S(1)}, bf16[128,1024]{1,0:T(8,128)(2,1)S(1)}, bf16[128,1024]{1,0:T(8,128)(2,1)S(1)}) custom-call(s32[2,256]{1,0:T(2,128)} %bitcast.2, bf16[256,1024]{1,0:T(8,128)(2,1)} %tokens_ref.3), custom_call_target="tpu_custom_call" | custom-call | flops 268435456 | bytes 1048576 | tf_op jit(solution)/shard_map/select/pallas_call | solution.py:161
  2.1 3.1 %collective-permute-start.2 = (bf16[128,1024]{1,0:T(8,128)(2,1)S(1)}, bf16[128,1024]{1,0:T(8,128)(2,1)S(1)}, u32[]{:S(2)}, u32[]{:S(2)}) collective-permute-start(bf16[128,1024]{1,0:T(8,128)(2,1)S(1)} %get-tuple-element.32), channel_id=1, source_target_pairs={{0,2},{1,3},{2,0},{3,1},{4,6},{5,7},{6,4},{7,5},{8,10},{9,11},{10,... | collective-permute-start | bytes 786440 | tf_op jit(solution)/shard_map/ppermute | solution.py:84
  5.1 2.6 %collective-permute-start.5 = (bf16[256,1024]{1,0:T(8,128)(2,1)}, bf16[256,1024]{1,0:T(8,128)(2,1)S(1)}, u32[]{:S(2)}, u32[]{:S(2)}) collective-permute-start(bf16[256,1024]{1,0:T(8,128)(2,1)} %tokens_ref.3), channel_id=1, source_target_pairs={{0,8},{1,9},{2,10},{3,11},{4,12},{5,13},{6,14},{7,15},{8,0},{9,1},... | collective-permute-start | bytes 1572872 | tf_op jit(solution)/shard_map/ppermute | solution.py:75
  8.1 2.9 %stage.1 = (bf16[1,1024,2048]{2,1,0:T(8,128)(2,1)S(1)}, bf16[1,1024,1024]{2,1,0:T(8,128)(2,1)S(1)}) custom-call(bf16[1,1024,2048]{2,1,0:T(8,128)(2,1)} %refs_0_.1, bf16[1,1024,1024]{2,1,0:T(8,128)(2,1)} %refs_1_.1, bf16[128,1024]{1,0:T(8,128)(2,1)S(1)} %get-tuple-element.31.refs_2_.refs_0_), custom_call_target="tpu_custom_call" | custom-call | bytes 12582912 | tf_op jit(solution)/shard_map/stage/pallas_call | solution.py:131
  11.6 2.8 %collective-permute-start.10 = (bf16[128,1024]{1,0:T(8,128)(2,1)S(1)}, bf16[128,1024]{1,0:T(8,128)(2,1)S(1)}, u32[]{:S(2)}, u32[]{:S(2)}) collective-permute-start(bf16[128,1024]{1,0:T(8,128)(2,1)S(1)} %get-tuple-element.41), channel_id=1, source_target_pairs={{0,6},{1,7},{2,4},{3,5},{4,2},{5,3},{6,0},{7,1},{8,14},{9,15},{10,... | collective-permute-start | bytes 786440 | tf_op jit(solution)/shard_map/ppermute | solution.py:84
  14.8 3.4 %shard_map.55 = (bf16[128,1024]{1,0:T(8,128)(2,1)S(1)}, bf16[128,1024]{1,0:T(8,128)(2,1)S(1)}) custom-call(bf16[128,1024]{1,0:T(8,128)(2,1)S(1)} %get-tuple-element.31.refs_2_.refs_0_, bf16[128,1024]{1,0:T(8,128)(2,1)S(1)} %collective-permute-done.2.refs_1_, bf16[1,1024,2048]{2,1,0:T(8,128)(2,1)S(1)} %get-tuple-element.33.refs_2_, ...), custom_call_target="tpu_custom_call" | custom-call | flops 3221225472 | bytes 1048576 | tf_op jit(solution)/shard_map/pallas_call | solution.py:332
  18.2 13.0 %collective-permute-done.routes_ref = s32[2,256]{1,0:T(2,128)S(1)} collective-permute-done((s32[2,256]{1,0:T(2,128)}, s32[2,256]{1,0:T(2,128)S(1)}, u32[]{:S(2)}, u32[]{:S(2)}) %collective-permute-start) | collective-permute-done | bytes 2080 | tf_op jit(solution)/shard_map/ppermute | solution.py:75
  32.5 0.7 collective-permute-start.6
  33.3 2.3 %collective-permute-start.7 = (bf16[128,1024]{1,0:T(8,128)(2,1)S(1)}, bf16[128,1024]{1,0:T(8,128)(2,1)S(1)}, u32[]{:S(2)}, u32[]{:S(2)}) collective-permute-start(bf16[128,1024]{1,0:T(8,128)(2,1)S(1)} %get-tuple-element.37), channel_id=1, source_target_pairs={{0,6},{1,7},{2,4},{3,5},{4,2},{5,3},{6,0},{7,1},{8,14},{9,15},{10,... | collective-permute-start | bytes 786440 | tf_op jit(solution)/shard_map/ppermute | solution.py:84
  35.6 2.2 %collective-permute-done.9.refs_0_ = bf16[128,1024]{1,0:T(8,128)(2,1)S(1)} collective-permute-done((bf16[128,1024]{1,0:T(8,128)(2,1)S(1)}, bf16[128,1024]{1,0:T(8,128)(2,1)S(1)}, u32[]{:S(2)}, u32[]{:S(2)}) %collective-permute-start.9) | collective-permute-done | bytes 262176 | tf_op jit(solution)/shard_map/ppermute | solution.py:84
  37.7 3.4 %shard_map.56 = (bf16[128,1024]{1,0:T(8,128)(2,1)S(1)}, bf16[128,1024]{1,0:T(8,128)(2,1)S(1)}) custom-call(bf16[128,1024]{1,0:T(8,128)(2,1)S(1)} %collective-permute-done.9.refs_0_, bf16[128,1024]{1,0:T(8,128)(2,1)S(1)} %collective-permute-done.10.refs_1_, bf16[1,1024,2048]{2,1,0:T(8,128)(2,1)S(1)} %get-tuple-element.33.refs_2_, ...), custom_call_target="tpu_custom_call" | custom-call | flops 3221225472 | bytes 1048576 | tf_op jit(solution)/shard_map/pallas_call | solution.py:332
  41.2 3.4 %shard_map.57 = (bf16[128,512]{1,0:T(8,128)(2,1)S(1)}, bf16[128,512]{1,0:T(8,128)(2,1)S(1)}, bf16[128,512]{1,0:T(8,128)(2,1)S(1)}, bf16[128,512]{1,0:T(8,128)(2,1)S(1)}) custom-call(bf16[128,1024]{1,0:T(8,128)(2,1)S(1)} %get-tuple-element.38.refs_6_.refs_0_, bf16[128,1024]{1,0:T(8,128)(2,1)S(1)} %collective-permute-done.8.refs_1_, ...), custom_call_target="tpu_custom_call" | custom-call | flops 3221225472 | bytes 1048576 | tf_op jit(solution)/shard_map/pallas_call | solution.py:332
  44.6 2.5 %collective-permute-done.7.refs_1_ = bf16[128,1024]{1,0:T(8,128)(2,1)S(1)} collective-permute-done((bf16[128,1024]{1,0:T(8,128)(2,1)S(1)}, bf16[128,1024]{1,0:T(8,128)(2,1)S(1)}, u32[]{:S(2)}, u32[]{:S(2)}) %collective-permute-start.7) | collective-permute-done | bytes 262176 | tf_op jit(solution)/shard_map/ppermute | solution.py:84
  47.1 2.9 %shard_map.58 = (bf16[128,512]{1,0:T(8,128)(2,1)S(1)}, bf16[128,512]{1,0:T(8,128)(2,1)S(1)}, bf16[256,1024]{1,0:T(8,128)(2,1)S(1)}, bf16[256,1024]{1,0:T(8,128)(2,1)S(1)}) custom-call(bf16[128,1024]{1,0:T(8,128)(2,1)S(1)} %collective-permute-done.6.refs_0_, bf16[128,1024]{1,0:T(8,128)(2,1)S(1)} %collective-permute-done.7.refs_1_, ...), custom_call_target="tpu_custom_call" | custom-call | flops 2684354560 | bytes 786432 | tf_op jit(solution)/shard_map/pallas_call | solution.py:332
  50.0 0.7 collective-permute-start.18
  50.8 2.3 %collective-permute-start.19 = (bf16[128,512]{1,0:T(8,128)(2,1)S(1)}, bf16[128,512]{1,0:T(8,128)(2,1)S(1)}, u32[]{:S(2)}, u32[]{:S(2)}) collective-permute-start(bf16[128,512]{1,0:T(8,128)(2,1)S(1)} %get-tuple-element.56), channel_id=1, source_target_pairs={{0,6},{1,7},{2,4},{3,5},{4,2},{5,3},{6,0},{7,1},{8,14},{9,15},{10,... | collective-permute-start | bytes 393224 | tf_op jit(solution)/shard_map/ppermute | solution.py:84
  54.3 0.7 collective-permute-start.12
  55.0 4.5 %collective-permute-start.1 = (f32[2,256]{1,0:T(2,128)S(1)}, f32[2,256]{1,0:T(2,128)S(1)}, u32[]{:S(2)}, u32[]{:S(2)}) collective-permute-start(f32[2,256]{1,0:T(2,128)S(1)} %bitcast.5), channel_id=1, source_target_pairs={{0,8},{1,9},{2,10},{3,11},{4,12},{5,13},{6,14},{7,15},{8,0},{9,1},... | collective-permute-start | bytes 6152 | tf_op jit(solution)/shard_map/ppermute | solution.py:75
  59.5 1.6 %collective-permute-done.1.gates_ref = f32[2,256]{1,0:T(2,128)S(1)} collective-permute-done((f32[2,256]{1,0:T(2,128)S(1)}, f32[2,256]{1,0:T(2,128)S(1)}, u32[]{:S(2)}, u32[]{:S(2)}) %collective-permute-start.1) | collective-permute-done | bytes 2080 | tf_op jit(solution)/shard_map/ppermute | solution.py:75
  61.1 3.4 %collective-permute-start.13 = (bf16[128,512]{1,0:T(8,128)(2,1)S(1)}, bf16[128,512]{1,0:T(8,128)(2,1)S(1)}, u32[]{:S(2)}, u32[]{:S(2)}) collective-permute-start(bf16[128,512]{1,0:T(8,128)(2,1)S(1)} %get-tuple-element.52), channel_id=1, source_target_pairs={{0,6},{1,7},{2,4},{3,5},{4,2},{5,3},{6,0},{7,1},{8,14},{9,15},{10,... | collective-permute-start | bytes 393224 | tf_op jit(solution)/shard_map/ppermute | solution.py:84
  64.5 0.9 collective-permute-start.11
  65.4 0.8 spread_gates.1
  66.2 2.6 %collective-permute-start.16 = (bf16[128,1024]{1,0:T(8,128)(2,1)S(1)}, bf16[128,1024]{1,0:T(8,128)(2,1)S(1)}, u32[]{:S(2)}, u32[]{:S(2)}) collective-permute-start(bf16[128,1024]{1,0:T(8,128)(2,1)S(1)} %get-tuple-element.54), channel_id=1, source_target_pairs={{0,6},{1,7},{2,4},{3,5},{4,2},{5,3},{6,0},{7,1},{8,14},{9,15},{10,... | collective-permute-start | bytes 786440 | tf_op jit(solution)/shard_map/ppermute | solution.py:84
  68.8 0.9 collective-permute-start.14
  70.2 1.2 %collective-permute-start.20 = (bf16[256,512]{1,0:T(8,128)(2,1)S(1)}, bf16[256,512]{1,0:T(8,128)(2,1)S(1)}, u32[]{:S(2)}, u32[]{:S(2)}) collective-permute-start(bf16[256,512]{1,0:T(8,128)(2,1)S(1)} %relay_sum.3), channel_id=1, source_target_pairs={{0,8},{1,9},{2,10},{3,11},{4,12},{5,13},{6,14},{7,15},{8,0},{9,1},... | collective-permute-start | bytes 786440 | tf_op jit(solution)/shard_map/ppermute | solution.py:75
  71.8 3.7 %collective-permute-start.21 = (bf16[256,512]{1,0:T(8,128)(2,1)S(1)}, bf16[256,512]{1,0:T(8,128)(2,1)S(1)}, u32[]{:S(2)}, u32[]{:S(2)}) collective-permute-start(bf16[256,512]{1,0:T(8,128)(2,1)S(1)} %relay_sum.2.after_ref), channel_id=1, source_target_pairs={{0,8},{1,9},{2,10},{3,11},{4,12},{5,13},{6,14},{7,15},{8,0},{9,1},... | collective-permute-start | bytes 786440 | tf_op jit(solution)/shard_map/ppermute | solution.py:75
  75.6 7.8 %collective-permute-done.15.refs_2_ = bf16[128,1024]{1,0:T(8,128)(2,1)S(1)} collective-permute-done((bf16[128,1024]{1,0:T(8,128)(2,1)S(1)}, bf16[128,1024]{1,0:T(8,128)(2,1)S(1)}, u32[]{:S(2)}, u32[]{:S(2)}) %collective-permute-start.15) | collective-permute-done | bytes 262176 | tf_op jit(solution)/shard_map/ppermute | solution.py:84
  83.3 3.2 %collective-permute-done.16.refs_3_ = bf16[128,1024]{1,0:T(8,128)(2,1)S(1)} collective-permute-done((bf16[128,1024]{1,0:T(8,128)(2,1)S(1)}, bf16[128,1024]{1,0:T(8,128)(2,1)S(1)}, u32[]{:S(2)}, u32[]{:S(2)}) %collective-permute-start.16) | collective-permute-done | bytes 262176 | tf_op jit(solution)/shard_map/ppermute | solution.py:84
  86.6 1.5 %near_sum.1.base_ref = f32[256,1024]{1,0:T(8,128)S(1)} custom-call(s32[2,256]{1,0:T(2,128)S(1)} %bitcast.4, f32[2,256]{1,0:T(2,128)S(1)} %bitcast.6, bf16[256,1024]{1,0:T(8,128)(2,1)S(1)} %copy-done, bf16[256,512]{1,0:T(8,128)(2,1)S(1)} %relay_sum.2.after_ref, bf16[128,1024]{1,0:T(8,128)(2,1)S(1)} %get-tuple-element.35.after_ref.refs_0_, ...), custom_call_target="tpu_custom_call" | custom-call | flops 536870912 | bytes 2621440 | tf_op jit(solution)/shard_map/near_sum/pallas_call | solution.py:264
  88.1 2.2 %collective-permute-done.20.refs_0_ = bf16[256,512]{1,0:T(8,128)(2,1)S(1)} collective-permute-done((bf16[256,512]{1,0:T(8,128)(2,1)S(1)}, bf16[256,512]{1,0:T(8,128)(2,1)S(1)}, u32[]{:S(2)}, u32[]{:S(2)}) %collective-permute-start.20) | collective-permute-done | bytes 262176 | tf_op jit(solution)/shard_map/ppermute | solution.py:75
  90.3 2.8 %collective-permute-done.21.refs_1_ = bf16[256,512]{1,0:T(8,128)(2,1)S(1)} collective-permute-done((bf16[256,512]{1,0:T(8,128)(2,1)S(1)}, bf16[256,512]{1,0:T(8,128)(2,1)S(1)}, u32[]{:S(2)}, u32[]{:S(2)}) %collective-permute-start.21) | collective-permute-done | bytes 262176 | tf_op jit(solution)/shard_map/ppermute | solution.py:75
  93.1 0.9 final_sum.1
  (32 shorter events, 5.4 us)
Async XLA Ops:
  0.0 14.8 %collective-permute-start.3 = (bf16[1,1024,2048]{2,1,0:T(8,128)(2,1)}, bf16[1,1024,2048]{2,1,0:T(8,128)(2,1)S(1)}, u32[]{:S(2)}, u32[]{:S(2)}) collective-permute-start(bf16[1,1024,2048]{2,1,0:T(8,128)(2,1)} %refs_0_.1), channel_id=1, source_target_pairs={{0,1},{1,0},{2,3},{3,2},{4,5},{5,4},{6,7},{7,6},{8,9},{9,8},{10,11... | collective-permute-start | bytes 12582920 | tf_op jit(solution)/shard_map/ppermute | solution.py:78
  0.5 13.9 %collective-permute-start.4 = (bf16[1,1024,1024]{2,1,0:T(8,128)(2,1)}, bf16[1,1024,1024]{2,1,0:T(8,128)(2,1)S(1)}, u32[]{:S(2)}, u32[]{:S(2)}) collective-permute-start(bf16[1,1024,1024]{2,1,0:T(8,128)(2,1)} %refs_1_.1), channel_id=1, source_target_pairs={{0,1},{1,0},{2,3},{3,2},{4,5},{5,4},{6,7},{7,6},{8,9},{9,8},{10,11... | collective-permute-start | bytes 6291464 | tf_op jit(solution)/shard_map/ppermute | solution.py:78
  2.1 9.5 %collective-permute-start.2 = (bf16[128,1024]{1,0:T(8,128)(2,1)S(1)}, bf16[128,1024]{1,0:T(8,128)(2,1)S(1)}, u32[]{:S(2)}, u32[]{:S(2)}) collective-permute-start(bf16[128,1024]{1,0:T(8,128)(2,1)S(1)} %get-tuple-element.32), channel_id=1, source_target_pairs={{0,2},{1,3},{2,0},{3,1},{4,6},{5,7},{6,4},{7,5},{8,10},{9,11},{10,... | collective-permute-start | bytes 786440 | tf_op jit(solution)/shard_map/ppermute | solution.py:84
  5.1 26.4 %collective-permute-start.5 = (bf16[256,1024]{1,0:T(8,128)(2,1)}, bf16[256,1024]{1,0:T(8,128)(2,1)S(1)}, u32[]{:S(2)}, u32[]{:S(2)}) collective-permute-start(bf16[256,1024]{1,0:T(8,128)(2,1)} %tokens_ref.3), channel_id=1, source_target_pairs={{0,8},{1,9},{2,10},{3,11},{4,12},{5,13},{6,14},{7,15},{8,0},{9,1},... | collective-permute-start | bytes 1572872 | tf_op jit(solution)/shard_map/ppermute | solution.py:75
  7.7 23.5 %collective-permute-start = (s32[2,256]{1,0:T(2,128)}, s32[2,256]{1,0:T(2,128)S(1)}, u32[]{:S(2)}, u32[]{:S(2)}) collective-permute-start(s32[2,256]{1,0:T(2,128)} %bitcast.3), channel_id=1, source_target_pairs={{0,8},{1,9},{2,10},{3,11},{4,12},{5,13},{6,14},{7,15},{8,0},{9,1},... | collective-permute-start | bytes 6152 | tf_op jit(solution)/shard_map/ppermute | solution.py:75
  11.6 24.0 %collective-permute-start.10 = (bf16[128,1024]{1,0:T(8,128)(2,1)S(1)}, bf16[128,1024]{1,0:T(8,128)(2,1)S(1)}, u32[]{:S(2)}, u32[]{:S(2)}) collective-permute-start(bf16[128,1024]{1,0:T(8,128)(2,1)S(1)} %get-tuple-element.41), channel_id=1, source_target_pairs={{0,6},{1,7},{2,4},{3,5},{4,2},{5,3},{6,0},{7,1},{8,14},{9,15},{10,... | collective-permute-start | bytes 786440 | tf_op jit(solution)/shard_map/ppermute | solution.py:84
  14.4 23.4 %collective-permute-start.9 = (bf16[128,1024]{1,0:T(8,128)(2,1)S(1)}, bf16[128,1024]{1,0:T(8,128)(2,1)S(1)}, u32[]{:S(2)}, u32[]{:S(2)}) collective-permute-start(bf16[128,1024]{1,0:T(8,128)(2,1)S(1)} %get-tuple-element.40), channel_id=1, source_target_pairs={{0,4},{1,5},{2,6},{3,7},{4,0},{5,1},{6,2},{7,3},{8,12},{9,13},{10,... | collective-permute-start | bytes 786440 | tf_op jit(solution)/shard_map/ppermute | solution.py:84
  32.0 9.2 %collective-permute-start.8 = (bf16[128,1024]{1,0:T(8,128)(2,1)S(1)}, bf16[128,1024]{1,0:T(8,128)(2,1)S(1)}, u32[]{:S(2)}, u32[]{:S(2)}) collective-permute-start(bf16[128,1024]{1,0:T(8,128)(2,1)S(1)} %get-tuple-element.39), channel_id=1, source_target_pairs={{0,2},{1,3},{2,0},{3,1},{4,6},{5,7},{6,4},{7,5},{8,10},{9,11},{10,... | collective-permute-start | bytes 786440 | tf_op jit(solution)/shard_map/ppermute | solution.py:84
  32.5 12.1 %collective-permute-start.6 = (bf16[128,1024]{1,0:T(8,128)(2,1)S(1)}, bf16[128,1024]{1,0:T(8,128)(2,1)S(1)}, u32[]{:S(2)}, u32[]{:S(2)}) collective-permute-start(bf16[128,1024]{1,0:T(8,128)(2,1)S(1)} %get-tuple-element.36), channel_id=1, source_target_pairs={{0,4},{1,5},{2,6},{3,7},{4,0},{5,1},{6,2},{7,3},{8,12},{9,13},{10,... | collective-permute-start | bytes 786440 | tf_op jit(solution)/shard_map/ppermute | solution.py:84
  33.3 13.8 %collective-permute-start.7 = (bf16[128,1024]{1,0:T(8,128)(2,1)S(1)}, bf16[128,1024]{1,0:T(8,128)(2,1)S(1)}, u32[]{:S(2)}, u32[]{:S(2)}) collective-permute-start(bf16[128,1024]{1,0:T(8,128)(2,1)S(1)} %get-tuple-element.37), channel_id=1, source_target_pairs={{0,6},{1,7},{2,4},{3,5},{4,2},{5,3},{6,0},{7,1},{8,14},{9,15},{10,... | collective-permute-start | bytes 786440 | tf_op jit(solution)/shard_map/ppermute | solution.py:84
  50.0 5.0 %copy-start.2 = (f32[256,2]{0,1:T(2,128)S(1)}, f32[256,2]{0,1:T(2,128)}, u32[]{:S(2)}) copy-start(f32[256,2]{0,1:T(2,128)} %param.7) | copy-start | bytes 6148
  50.0 36.6 %copy-start = (bf16[256,1024]{1,0:T(8,128)(2,1)S(1)}, bf16[256,1024]{1,0:T(8,128)(2,1)}, u32[]{:S(2)}) copy-start(bf16[256,1024]{1,0:T(8,128)(2,1)} %tokens_ref.3) | copy-start | bytes 1572868
  50.0 36.5 %copy-start.1 = (s32[256,2]{0,1:T(2,128)S(1)}, s32[256,2]{0,1:T(2,128)}, u32[]{:S(2)}) copy-start(s32[256,2]{0,1:T(2,128)} %param.6) | copy-start | bytes 6148
  50.0 14.4 %collective-permute-start.18 = (bf16[128,512]{1,0:T(8,128)(2,1)S(1)}, bf16[128,512]{1,0:T(8,128)(2,1)S(1)}, u32[]{:S(2)}, u32[]{:S(2)}) collective-permute-start(bf16[128,512]{1,0:T(8,128)(2,1)S(1)} %get-tuple-element.44.after_ref), channel_id=1, source_target_pairs={{0,4},{1,5},{2,6},{3,7},{4,0},{5,1},{6,2},{7,3},{8,12},{9,13},{10,... | collective-permute-start | bytes 393224 | tf_op jit(solution)/shard_map/ppermute | solution.py:84
  50.8 15.4 %collective-permute-start.19 = (bf16[128,512]{1,0:T(8,128)(2,1)S(1)}, bf16[128,512]{1,0:T(8,128)(2,1)S(1)}, u32[]{:S(2)}, u32[]{:S(2)}) collective-permute-start(bf16[128,512]{1,0:T(8,128)(2,1)S(1)} %get-tuple-element.56), channel_id=1, source_target_pairs={{0,6},{1,7},{2,4},{3,5},{4,2},{5,3},{6,0},{7,1},{8,14},{9,15},{10,... | collective-permute-start | bytes 393224 | tf_op jit(solution)/shard_map/ppermute | solution.py:84
  53.1 13.2 %collective-permute-start.17 = (bf16[128,512]{1,0:T(8,128)(2,1)S(1)}, bf16[128,512]{1,0:T(8,128)(2,1)S(1)}, u32[]{:S(2)}, u32[]{:S(2)}) collective-permute-start(bf16[128,512]{1,0:T(8,128)(2,1)S(1)} %get-tuple-element.55), channel_id=1, source_target_pairs={{0,2},{1,3},{2,0},{3,1},{4,6},{5,7},{6,4},{7,5},{8,10},{9,11},{10,... | collective-permute-start | bytes 393224 | tf_op jit(solution)/shard_map/ppermute | solution.py:84
  54.3 14.5 %collective-permute-start.12 = (bf16[128,512]{1,0:T(8,128)(2,1)S(1)}, bf16[128,512]{1,0:T(8,128)(2,1)S(1)}, u32[]{:S(2)}, u32[]{:S(2)}) collective-permute-start(bf16[128,512]{1,0:T(8,128)(2,1)S(1)} %get-tuple-element.51), channel_id=1, source_target_pairs={{0,4},{1,5},{2,6},{3,7},{4,0},{5,1},{6,2},{7,3},{8,12},{9,13},{10,... | collective-permute-start | bytes 393224 | tf_op jit(solution)/shard_map/ppermute | solution.py:84
  55.0 6.1 %collective-permute-start.1 = (f32[2,256]{1,0:T(2,128)S(1)}, f32[2,256]{1,0:T(2,128)S(1)}, u32[]{:S(2)}, u32[]{:S(2)}) collective-permute-start(f32[2,256]{1,0:T(2,128)S(1)} %bitcast.5), channel_id=1, source_target_pairs={{0,8},{1,9},{2,10},{3,11},{4,12},{5,13},{6,14},{7,15},{8,0},{9,1},... | collective-permute-start | bytes 6152 | tf_op jit(solution)/shard_map/ppermute | solution.py:75
  61.1 9.0 %collective-permute-start.13 = (bf16[128,512]{1,0:T(8,128)(2,1)S(1)}, bf16[128,512]{1,0:T(8,128)(2,1)S(1)}, u32[]{:S(2)}, u32[]{:S(2)}) collective-permute-start(bf16[128,512]{1,0:T(8,128)(2,1)S(1)} %get-tuple-element.52), channel_id=1, source_target_pairs={{0,6},{1,7},{2,4},{3,5},{4,2},{5,3},{6,0},{7,1},{8,14},{9,15},{10,... | collective-permute-start | bytes 393224 | tf_op jit(solution)/shard_map/ppermute | solution.py:84
  64.5 6.9 %collective-permute-start.11 = (bf16[128,512]{1,0:T(8,128)(2,1)S(1)}, bf16[128,512]{1,0:T(8,128)(2,1)S(1)}, u32[]{:S(2)}, u32[]{:S(2)}) collective-permute-start(bf16[128,512]{1,0:T(8,128)(2,1)S(1)} %get-tuple-element.48), channel_id=1, source_target_pairs={{0,2},{1,3},{2,0},{3,1},{4,6},{5,7},{6,4},{7,5},{8,10},{9,11},{10,... | collective-permute-start | bytes 393224 | tf_op jit(solution)/shard_map/ppermute | solution.py:84
  66.1 17.2 %collective-permute-start.15 = (bf16[128,1024]{1,0:T(8,128)(2,1)S(1)}, bf16[128,1024]{1,0:T(8,128)(2,1)S(1)}, u32[]{:S(2)}, u32[]{:S(2)}) collective-permute-start(bf16[128,1024]{1,0:T(8,128)(2,1)S(1)} %get-tuple-element.42.refs_6_), channel_id=1, source_target_pairs={{0,4},{1,5},{2,6},{3,7},{4,0},{5,1},{6,2},{7,3},{8,12},{9,13},{10,... | collective-permute-start | bytes 786440 | tf_op jit(solution)/shard_map/ppermute | solution.py:84
  66.2 20.3 %collective-permute-start.16 = (bf16[128,1024]{1,0:T(8,128)(2,1)S(1)}, bf16[128,1024]{1,0:T(8,128)(2,1)S(1)}, u32[]{:S(2)}, u32[]{:S(2)}) collective-permute-start(bf16[128,1024]{1,0:T(8,128)(2,1)S(1)} %get-tuple-element.54), channel_id=1, source_target_pairs={{0,6},{1,7},{2,4},{3,5},{4,2},{5,3},{6,0},{7,1},{8,14},{9,15},{10,... | collective-permute-start | bytes 786440 | tf_op jit(solution)/shard_map/ppermute | solution.py:84
  68.8 17.7 %collective-permute-start.14 = (bf16[128,1024]{1,0:T(8,128)(2,1)S(1)}, bf16[128,1024]{1,0:T(8,128)(2,1)S(1)}, u32[]{:S(2)}, u32[]{:S(2)}) collective-permute-start(bf16[128,1024]{1,0:T(8,128)(2,1)S(1)} %get-tuple-element.53), channel_id=1, source_target_pairs={{0,2},{1,3},{2,0},{3,1},{4,6},{5,7},{6,4},{7,5},{8,10},{9,11},{10,... | collective-permute-start | bytes 786440 | tf_op jit(solution)/shard_map/ppermute | solution.py:84
  70.2 20.1 %collective-permute-start.20 = (bf16[256,512]{1,0:T(8,128)(2,1)S(1)}, bf16[256,512]{1,0:T(8,128)(2,1)S(1)}, u32[]{:S(2)}, u32[]{:S(2)}) collective-permute-start(bf16[256,512]{1,0:T(8,128)(2,1)S(1)} %relay_sum.3), channel_id=1, source_target_pairs={{0,8},{1,9},{2,10},{3,11},{4,12},{5,13},{6,14},{7,15},{8,0},{9,1},... | collective-permute-start | bytes 786440 | tf_op jit(solution)/shard_map/ppermute | solution.py:75
  71.8 21.2 %collective-permute-start.21 = (bf16[256,512]{1,0:T(8,128)(2,1)S(1)}, bf16[256,512]{1,0:T(8,128)(2,1)S(1)}, u32[]{:S(2)}, u32[]{:S(2)}) collective-permute-start(bf16[256,512]{1,0:T(8,128)(2,1)S(1)} %relay_sum.2.after_ref), channel_id=1, source_target_pairs={{0,8},{1,9},{2,10},{3,11},{4,12},{5,13},{6,14},{7,15},{8,0},{9,1},... | collective-permute-start | bytes 786440 | tf_op jit(solution)/shard_map/ppermute | solution.py:75
